TPU v7x, 512 devices: a whole 4x4x16 slice. The times are simulated.
512 devices in a mesh: tm: 32 (over x, z_lo), height: 8 (over z_hi, y), dp: 2 (over core).
Axes of the slice: x: 4, y: 4, z: 16 (z_hi: 2, z_lo: 8; z = z_hi * 8 + z_lo), core: 2. Of those that a mesh axis runs over, the one named last changes fastest.
Arguments:
- frames_in: bfloat16 [2, 128, 32, 48, 256], P('dp', 'tm', 'height'), may hold values from -6 to 6
- cotangent: bfloat16 [2, 128, 32, 48, 256], P('dp', 'tm', 'height'), may hold values from -6 to 6
- w_spatial: bfloat16 [3, 3, 256, 256], replicated, may hold values from -0.125 to 0.125
- w_temporal: bfloat16 [3, 256, 256], replicated, may hold values from -0.21875 to 0.21875
Outputs:
- decoded: bfloat16 [2, 128, 32, 48, 256], P('dp', 'tm', 'height')
- input_grad: bfloat16 [2, 128, 32, 48, 256], P('dp', 'tm', 'height')
- spatial_grad: bfloat16 [3, 3, 256, 256], replicated
- temporal_grad: bfloat16 [3, 256, 256], replicated
All inputs are finite; a program needn't handle non-finite values.
Results may differ from a plain program's by a relative error of at most 0.0061.
Values may be sent and summed in bfloat16 or wider, within the bound.
No kernel may reach another device: no remote copies, remote signals or barrier semaphores. Data moves between devices by JAX's collectives and lax.ppermute only.
A program may use at most 64 MiB of HBM per device.

v0:
```python
import math
import jax
import jax.numpy as jnp
from jax import lax
from jax.sharding import PartitionSpec as P


def extended(x, sides, width):
    for axis, dim in sides:
        count, length = (lax.axis_size(axis), x.shape[dim])
        up = [(i, (i + 1) % count) for i in range(count - 1)]
        down = [(j, i) for i, j in up]
        last = lax.slice_in_dim(x, length - width, length, axis=dim)
        initial = lax.slice_in_dim(x, 0, width, axis=dim)
        before = lax.ppermute(last, axis, up)
        after = lax.ppermute(initial, axis, down)
        x = jnp.concatenate([before, x, after], axis=dim)
    return x


def from_behind(block, axis, distance):
    devices = range(lax.axis_size(axis))
    route = [(i - distance, i) for i in devices if i - distance in devices]
    return lax.ppermute(block, axis, route)


def silu_slope(values):
    sigmoid_value = jax.nn.sigmoid(values)
    return sigmoid_value * (1.0 + values * (1.0 - sigmoid_value))


def frame_taps(source, frame_count):
    return jnp.concatenate(
        [source[shift_tap : shift_tap + frame_count] for shift_tap in range(3)], axis=-1
    )


def flat_dot(left_side, right_side):
    return jnp.dot(
        left_side.reshape(-1, left_side.shape[-1]), right_side, preferred_element_type=jnp.float32
    )


def local(frames_in, cotangent, w_spatial, w_temporal):
    inputs = frames_in[0]
    upstream = cotangent[0]
    frame_count, row_count, col_count, channels = inputs.shape
    temporal_flat = w_temporal.reshape(3 * channels, channels)
    temporal_back = jnp.concatenate([w_temporal[2].T, w_temporal[1].T, w_temporal[0].T], axis=0)
    first_shard = lax.axis_index("tm") == 0
    activated = jax.nn.silu(inputs.astype(jnp.float32)).astype(jnp.bfloat16)
    activ_rows = extended(activated, (("height", 1),), 1)
    activ_pad = jnp.pad(activ_rows, ((0, 0), (0, 0), (1, 1), (0, 0)))
    spatial_out = lax.conv_general_dilated(
        activ_pad,
        w_spatial,
        (1, 1),
        "VALID",
        dimension_numbers=("NHWC", "HWIO", "NHWC"),
        preferred_element_type=jnp.float32,
    ).astype(jnp.bfloat16)
    earlier = from_behind(spatial_out[frame_count - 2 :], "tm", 1)
    repeated = jnp.broadcast_to(spatial_out[:1], earlier.shape)
    earlier = jnp.where(first_shard, repeated, earlier)
    padded_frames = jnp.concatenate([earlier, spatial_out], axis=0)
    frame_stack = frame_taps(padded_frames, frame_count).reshape(-1, 3 * channels)
    temporal_out = jnp.dot(frame_stack, temporal_flat, preferred_element_type=jnp.float32).reshape(
        inputs.shape
    )
    decoded = (inputs.astype(jnp.float32) + temporal_out).astype(jnp.bfloat16)
    upstream_ext = jnp.pad(upstream, ((2, 2), (0, 0), (0, 0), (0, 0)))
    frame_part = flat_dot(frame_taps(upstream_ext, frame_count + 2), temporal_back)
    frame_part = frame_part.reshape(frame_count + 2, row_count, col_count, channels)
    rim_part = frame_part[:2]
    returned = from_behind(rim_part, "tm", -1)
    frame_sum = frame_part[2:]
    frame_sum = frame_sum.at[frame_count - 2 :].add(returned)
    frame_sum = frame_sum.at[0].add(jnp.where(first_shard, rim_part[0] + rim_part[1], 0.0))
    frame_grad = frame_sum.astype(jnp.bfloat16)
    grad_pad = jnp.pad(frame_grad, ((0, 0), (2, 2), (1, 1), (0, 0)))
    spatial_flip = jnp.flip(w_spatial, (0, 1)).transpose(0, 1, 3, 2)
    grad_ext = lax.conv_general_dilated(
        grad_pad,
        spatial_flip,
        (1, 1),
        "VALID",
        dimension_numbers=("NHWC", "HWIO", "NHWC"),
        preferred_element_type=jnp.float32,
    )
    edge_rows = jnp.stack([grad_ext[:, 0], grad_ext[:, row_count + 1]], axis=1)
    arrived = extended(edge_rows.astype(jnp.bfloat16), (("height", 1),), 1).astype(edge_rows.dtype)
    act_grad = grad_ext[:, 1 : row_count + 1]
    act_grad = act_grad.at[:, 0].add(arrived[:, 0])
    act_grad = act_grad.at[:, row_count - 1].add(arrived[:, 3])
    input_grad = (
        upstream.astype(jnp.float32) + silu_slope(inputs.astype(jnp.float32)) * act_grad
    ).astype(jnp.bfloat16)
    cell_count = (
        frame_count
        * lax.axis_size("tm")
        * row_count
        * lax.axis_size("height")
        * col_count
        * lax.axis_size("dp")
    )
    grad_scale = 1.0 / math.sqrt(cell_count)
    contract = (((0,), (0,)), ((), ()))
    spatial_term = lax.conv_general_dilated(
        activ_pad,
        frame_grad,
        (1, 1),
        "VALID",
        dimension_numbers=("CHWN", "IHWO", "HWNC"),
        preferred_element_type=jnp.float32,
    ).reshape(9 * channels, channels)
    temporal_term = lax.dot_general(
        frame_stack, upstream.reshape(-1, channels), contract, preferred_element_type=jnp.float32
    )
    weight_terms = jnp.concatenate([spatial_term, temporal_term], axis=0) * grad_scale
    summed = lax.psum(weight_terms, ("tm", "height", "dp")).astype(jnp.bfloat16)
    spatial_grad = summed[: 9 * channels].reshape(3, 3, channels, channels)
    temporal_grad = summed[9 * channels :].reshape(3, channels, channels)
    return (decoded[None], input_grad[None], spatial_grad, temporal_grad)


def solution(mesh):
    return jax.shard_map(
        local,
        mesh=mesh,
        in_specs=(
            P("dp", "tm", "height", None, None),
            P("dp", "tm", "height", None, None),
            P(),
            P(),
        ),
        out_specs=(
            P("dp", "tm", "height", None, None),
            P("dp", "tm", "height", None, None),
            P(),
            P(),
        ),
        check_vma=False,
    )
```

profile of v0, /device:TPU:32, one launch (start us, length us, event | category | flops | bytes accessed | tf_op | source)
XLA Modules:
  0.0 292.8 jit_solution(13264414294264656128)
XLA Ops:
  0.6 1.2 slice_bitcast_fusion.2
  1.8 1.5 pad_slice_fusion.2
  5.3 7.4 %collective-permute-start.3 = (f32[2,4,48,256]{3,0,2,1:T(2,128)}, f32[2,4,48,256]{3,0,2,1:T(2,128)}, u32[]{:S(2)}, u32[]{:S(2)}) collective-permute-start(f32[2,4,48,256]{3,0,2,1:T(2,128)} %copy.24), channel_id=1, source_target_pairs={{16,0},{32,16},{48,32},{64,48},{80,64},{96,80},{112,96},{128,112},... | collective-permute-start | bytes 1179656 | tf_op jit(solution)/shard_map/ppermute | solution.py:24
  13.6 1.6 copy.26
  15.3 3.2 %collective-permute-done.3 = f32[2,4,48,256]{3,0,2,1:T(2,128)} collective-permute-done((f32[2,4,48,256]{3,0,2,1:T(2,128)}, f32[2,4,48,256]{3,0,2,1:T(2,128)}, u32[]{:S(2)}, u32[]{:S(2)}) %collective-permute-start.3) | collective-permute-done | bytes 393248 | tf_op jit(solution)/shard_map/ppermute | solution.py:24
  18.5 1.5 fusion.34
  20.3 6.3 %scatter-add.15 = f32[4,4,48,256]{3,0,2,1:T(4,128)S(1)} dynamic-update-slice(f32[4,4,48,256]{3,0,2,1:T(4,128)S(1)} %fusion.34, f32[1,4,48,256]{3,0,2,1:T(1,128)S(1)} %slice_add_fusion.2, s32[]{:T(128)} %constant.118.clone.1, s32[]{:T(128)} %constant.118.clone.1, s32[]{:T(128)} %constant.118.clone.1, s32[]{:T(128)} %constant.118.clone.1) | dynamic-update-slice | bytes 393220 | tf_op jit(solution)/shard_map/scatter-add | solution.py:78
  27.1 1.8 fusion.50
  31.3 4.1 %collective-permute-start.4 = (bf16[4,1,48,256]{3,2,1,0:T(8,128)(2,1)S(1)}, bf16[4,1,48,256]{3,2,1,0:T(8,128)(2,1)}, u32[]{:S(2)}, u32[]{:S(2)}) collective-permute-start(bf16[4,1,48,256]{3,2,1,0:T(8,128)(2,1)S(1)} %slice_bitcast_fusion.4), channel_id=1, source_target_pairs={{0,2},{2,4},{4,6},{6,8},{8,10},{10,12},{12,14},{1,3},{3,5},{5,7},{... | collective-permute-start | bytes 294920 | tf_op jit(solution)/shard_map/ppermute | solution.py:15
  35.4 1.6 copy.35
  38.0 1.3 collective-permute-start.5
  40.7 3.8 %collective-permute-done.5 = bf16[4,1,48,256]{3,2,1,0:T(8,128)(2,1)S(1)} collective-permute-done((bf16[4,1,48,256]{3,2,1,0:T(8,128)(2,1)S(1)}, bf16[4,1,48,256]{3,2,1,0:T(8,128)(2,1)S(1)}, u32[]{:S(2)}, u32[]{:S(2)}) %collective-permute-start.5) | collective-permute-done | bytes 98336 | tf_op jit(solution)/shard_map/ppermute | solution.py:16
  45.5 1.1 fusion.35
  46.6 2.9 collective-permute-start
  49.5 1.3 collective-permute-start.1
  51.7 14.0 %collective-permute-done.1 = bf16[4,1,48,256]{3,2,1,0:T(8,128)(2,1)S(1)} collective-permute-done((bf16[4,1,48,256]{3,2,1,0:T(8,128)(2,1)S(1)}, bf16[4,1,48,256]{3,2,1,0:T(8,128)(2,1)S(1)}, u32[]{:S(2)}, u32[]{:S(2)}) %collective-permute-start.1) | collective-permute-done | bytes 98336 | tf_op jit(solution)/shard_map/ppermute | solution.py:16
  66.9 1.2 fusion.1
  68.7 3.1 %collective-permute-start.2 = (bf16[2,4,48,256]{3,2,1,0:T(8,128)(2,1)S(1)}, bf16[2,4,48,256]{3,2,1,0:T(8,128)(2,1)S(1)}, u32[]{:S(2)}, u32[]{:S(2)}) collective-permute-start(bf16[2,4,48,256]{3,2,1,0:T(8,128)(2,1)S(1)} %slice.241), channel_id=1, source_target_pairs={{0,16},{16,32},{32,48},{48,64},{64,80},{80,96},{96,112},{112,128},... | collective-permute-start | bytes 589832 | tf_op jit(solution)/shard_map/ppermute | solution.py:24
  71.9 2.1 fusion.25
  74.0 2.3 collective-permute-done.2
  77.1 2.0 maximum_multiply_fusion
  79.1 210.6 %all-reduce.2 = bf16[3072,256]{1,0:T(8,128)(2,1)S(1)} all-reduce(f32[3072,256]{1,0:T(8,128)} %maximum_multiply_fusion), channel_id=1, replica_groups=mesh['tm'=32,'height'=8,'dp'=2] {'tm','height','dp'}, use_global_device_ids=true, to_apply=%region_0.1 | all-reduce | flops 786432 | bytes 4718592 | tf_op jit(solution)/shard_map/psum | solution.py:120
  290.5 1.1 slice.260
  291.6 1.2 fusion.3
  (62 shorter events, 13.4 us)
Async XLA Ops:
  0.6 26.5 %copy-start = (bf16[3,3,256,256]{3,2,1,0:T(8,128)(2,1)S(1)}, bf16[3,3,256,256]{3,2,1,0:T(8,128)(2,1)}, u32[]{:S(2)}) copy-start(bf16[3,3,256,256]{3,2,1,0:T(8,128)(2,1)} %param.14) | copy-start | bytes 3538948
  5.3 13.2 %collective-permute-start.3 = (f32[2,4,48,256]{3,0,2,1:T(2,128)}, f32[2,4,48,256]{3,0,2,1:T(2,128)}, u32[]{:S(2)}, u32[]{:S(2)}) collective-permute-start(f32[2,4,48,256]{3,0,2,1:T(2,128)} %copy.24), channel_id=1, source_target_pairs={{16,0},{32,16},{48,32},{64,48},{80,64},{96,80},{112,96},{128,112},... | collective-permute-start | bytes 1179656 | tf_op jit(solution)/shard_map/ppermute | solution.py:24
  20.3 6.8 %copy-start.7 = (pred[32,7]{0,1:T(8,128)(4,1)S(1)}, pred[32,7]{0,1:T(8,128)(4,1)}, u32[]{:S(2)}) copy-start(pred[32,7]{0,1:T(8,128)(4,1)} %constant.137) | copy-start | bytes 676
  31.3 9.4 %collective-permute-start.4 = (bf16[4,1,48,256]{3,2,1,0:T(8,128)(2,1)S(1)}, bf16[4,1,48,256]{3,2,1,0:T(8,128)(2,1)}, u32[]{:S(2)}, u32[]{:S(2)}) collective-permute-start(bf16[4,1,48,256]{3,2,1,0:T(8,128)(2,1)S(1)} %slice_bitcast_fusion.4), channel_id=1, source_target_pairs={{0,2},{2,4},{4,6},{6,8},{8,10},{10,12},{12,14},{1,3},{3,5},{5,7},{... | collective-permute-start | bytes 294920 | tf_op jit(solution)/shard_map/ppermute | solution.py:15
  38.0 6.5 %collective-permute-start.5 = (bf16[4,1,48,256]{3,2,1,0:T(8,128)(2,1)S(1)}, bf16[4,1,48,256]{3,2,1,0:T(8,128)(2,1)S(1)}, u32[]{:S(2)}, u32[]{:S(2)}) collective-permute-start(bf16[4,1,48,256]{3,2,1,0:T(8,128)(2,1)S(1)} %slice_bitcast_fusion.3), channel_id=1, source_target_pairs={{2,0},{4,2},{6,4},{8,6},{10,8},{12,10},{14,12},{3,1},{5,3},{7,5},{... | collective-permute-start | bytes 294920 | tf_op jit(solution)/shard_map/ppermute | solution.py:16
  40.1 5.3 %copy-start.1 = (bf16[1,4,4,48,256]{4,3,2,1,0:T(8,128)(2,1)S(1)}, bf16[1,4,4,48,256]{4,3,2,1,0:T(8,128)(2,1)}, u32[]{:S(2)}) copy-start(bf16[1,4,4,48,256]{4,3,2,1,0:T(8,128)(2,1)} %param.13) | copy-start | bytes 1179652
  40.2 5.3 %copy-start.4 = (bf16[1,4,4,48,256]{4,3,2,1,0:T(8,128)(2,1)S(1)}, bf16[1,4,4,48,256]{4,3,2,1,0:T(8,128)(2,1)}, u32[]{:S(2)}) copy-start(bf16[1,4,4,48,256]{4,3,2,1,0:T(8,128)(2,1)} %param.12) | copy-start | bytes 1179652
  46.6 5.1 %collective-permute-start = (bf16[4,1,48,256]{3,2,1,0:T(8,128)(2,1)S(1)}, bf16[4,1,48,256]{3,2,1,0:T(8,128)(2,1)S(1)}, u32[]{:S(2)}, u32[]{:S(2)}) collective-permute-start(bf16[4,1,48,256]{3,2,1,0:T(8,128)(2,1)S(1)} %get-tuple-element.66), channel_id=1, source_target_pairs={{0,2},{2,4},{4,6},{6,8},{8,10},{10,12},{12,14},{1,3},{3,5},{5,7},{... | collective-permute-start | bytes 294920 | tf_op jit(solution)/shard_map/ppermute | solution.py:15
  49.5 16.2 %collective-permute-start.1 = (bf16[4,1,48,256]{3,2,1,0:T(8,128)(2,1)S(1)}, bf16[4,1,48,256]{3,2,1,0:T(8,128)(2,1)S(1)}, u32[]{:S(2)}, u32[]{:S(2)}) collective-permute-start(bf16[4,1,48,256]{3,2,1,0:T(8,128)(2,1)S(1)} %get-tuple-element.67), channel_id=1, source_target_pairs={{2,0},{4,2},{6,4},{8,6},{10,8},{12,10},{14,12},{3,1},{5,3},{7,5},{... | collective-permute-start | bytes 294920 | tf_op jit(solution)/shard_map/ppermute | solution.py:16
  66.2 0.7 copy-start.8
  68.7 7.6 %collective-permute-start.2 = (bf16[2,4,48,256]{3,2,1,0:T(8,128)(2,1)S(1)}, bf16[2,4,48,256]{3,2,1,0:T(8,128)(2,1)S(1)}, u32[]{:S(2)}, u32[]{:S(2)}) collective-permute-start(bf16[2,4,48,256]{3,2,1,0:T(8,128)(2,1)S(1)} %slice.241), channel_id=1, source_target_pairs={{0,16},{16,32},{32,48},{48,64},{64,80},{80,96},{96,112},{112,128},... | collective-permute-start | bytes 589832 | tf_op jit(solution)/shard_map/ppermute | solution.py:24
  76.4 0.7 copy-start.2
  289.7 1.9 copy-start.3
  289.7 1.9 copy-start.5
  289.7 1.9 copy-start.6
where the time goes:
time: 293 us
  blocking collectives  211 us (72%)
  waiting for transfers between devices  24.2 us (8%)
  local copies, waits for them, and re-layouts  22.6 us (8%)
  starting transfers between devices  20 us (7%)
  matrix products  7.58 us (3%)
  other arithmetic  6.71 us (2%)
    psum x1, blocking collectives, local(): summed = lax.psum(weight_terms, ('tm', 'height', 'dp')).astype(jnp.bfloat16)  211 us
    ppermute x2, waiting for transfers between devices, extended(): after = lax.ppermute(initial, axis, down)  17.7 us
    ppermute x2, starting transfers between devices, from_behind(): return lax.ppermute(block, axis, route)  10.5 us
    ppermute x2, starting transfers between devices, extended(): before = lax.ppermute(last, axis, up)  6.98 us
    scatter-add x1, local copies, waits for them, and re-layouts, local(): frame_sum.at[0].add(jnp.where(first_shard, rim_part[0] + rim_part[1], 0.0))  6.33 us
  transfers between devices with their start and end apart: 6, of which 5 were waited for; matrix products, arithmetic and copies ran while one was open for 3% of the time, Pallas kernels for 0%

commit v1 on v0

--- a/solution.py
+++ b/solution.py
@@ -117,7 +117,7 @@
         frame_stack, upstream.reshape(-1, channels), contract, preferred_element_type=jnp.float32
     )
     weight_terms = jnp.concatenate([spatial_term, temporal_term], axis=0) * grad_scale
-    summed = lax.psum(weight_terms, ("tm", "height", "dp")).astype(jnp.bfloat16)
+    summed = lax.psum(lax.psum(weight_terms, "tm"), ("height", "dp")).astype(jnp.bfloat16)
     spatial_grad = summed[: 9 * channels].reshape(3, 3, channels, channels)
     temporal_grad = summed[9 * channels :].reshape(3, channels, channels)
     return (decoded[None], input_grad[None], spatial_grad, temporal_grad)

time: 293 us -> 780 us (2.66)
  the two profiles are of different devices: /device:TPU:32 before, /device:TPU:223 now
where the time goes in v1:
time: 780 us; the launch traced here: 779 us
  waiting for transfers between devices  490 us (63%)
  blocking collectives  218 us (28%)
  local copies, waits for them, and re-layouts  23.5 us (3%)
  starting transfers between devices  19.7 us (3%)
  between operations  14.5 us (2%)
    psum x1, waiting for transfers between devices, local(): lax.psum(weight_terms, 'tm')  452 us
    psum x1, blocking collectives, local(): lax.psum(lax.psum(weight_terms, 'tm'), ('height', 'dp'))  218 us
    ppermute x2, waiting for transfers between devices, extended(): after = lax.ppermute(initial, axis, down)  27.6 us
  transfers between devices with their start and end apart: 7, of which 6 were waited for; matrix products, arithmetic and copies ran while one was open for 1% of the time, Pallas kernels for 0%

profile of v1, /device:TPU:223, one launch (start us, length us, event | category | flops | bytes accessed | tf_op | source)
XLA Modules:
  0.0 779.3 jit_solution(16309484708782675760)
XLA Ops:
  7.2 1.1 slice_bitcast_fusion.2
  8.4 1.6 pad_slice_fusion.2
  11.9 1.9 collective-permute-start.3
  14.7 1.6 copy.26
  16.4 7.6 collective-permute-done.3
  24.1 1.5 fusion.34
  25.9 6.3 scatter-add.15
  32.7 1.8 fusion.50
  36.8 8.5 %collective-permute-start.4 = (bf16[4,1,48,256]{3,2,1,0:T(8,128)(2,1)S(1)}, bf16[4,1,48,256]{3,2,1,0:T(8,128)(2,1)}, u32[]{:S(2)}, u32[]{:S(2)}) collective-permute-start(bf16[4,1,48,256]{3,2,1,0:T(8,128)(2,1)S(1)} %slice_bitcast_fusion.4), channel_id=1, source_target_pairs={{0,2},{2,4},{4,6},{6,8},{8,10},{10,12},{12,14},{1,3},{3,5},{5,7},{... | collective-permute-start | bytes 294920 | tf_op jit(solution)/shard_map/ppermute | solution.py:15
  45.3 1.6 copy.35
  47.9 1.9 collective-permute-start.5
  51.3 13.9 %collective-permute-done.5 = bf16[4,1,48,256]{3,2,1,0:T(8,128)(2,1)S(1)} collective-permute-done((bf16[4,1,48,256]{3,2,1,0:T(8,128)(2,1)S(1)}, bf16[4,1,48,256]{3,2,1,0:T(8,128)(2,1)S(1)}, u32[]{:S(2)}, u32[]{:S(2)}) %collective-permute-start.5) | collective-permute-done | bytes 98336 | tf_op jit(solution)/shard_map/ppermute | solution.py:16
  66.2 1.1 fusion.35
  67.3 1.9 collective-permute-start
  69.2 3.4 collective-permute-start.1
  72.7 13.7 %collective-permute-done.1 = bf16[4,1,48,256]{3,2,1,0:T(8,128)(2,1)S(1)} collective-permute-done((bf16[4,1,48,256]{3,2,1,0:T(8,128)(2,1)S(1)}, bf16[4,1,48,256]{3,2,1,0:T(8,128)(2,1)S(1)}, u32[]{:S(2)}, u32[]{:S(2)}) %collective-permute-start.1) | collective-permute-done | bytes 98336 | tf_op jit(solution)/shard_map/ppermute | solution.py:16
  87.7 1.2 fusion.1
  89.5 2.1 collective-permute-start.2
  91.6 2.0 fusion.25
  93.6 2.3 collective-permute-done.2
  96.6 2.0 maximum_multiply_fusion
  99.6 1.2 fusion.3
  100.8 452.0 %all-reduce.4.cloned.1.call-done = f32[3072,256]{1,0:T(8,128)} async-done(((f32[3072,256]{1,0:T(8,128)}), f32[3072,256]{1,0:T(8,128)}) %all-reduce.4.cloned.1.call-update) | async-done | bytes 3145744 | tf_op jit(solution)/shard_map/psum | solution.py:120
  552.8 217.8 %all-reduce.5 = bf16[3072,256]{1,0:T(8,128)(2,1)S(1)} all-reduce(f32[3072,256]{1,0:T(8,128)} %all-reduce.4.cloned.1.call-done), channel_id=1, replica_groups=mesh['tm'=32,'height'=8,'dp'=2] {'height','dp'}, use_global_device_ids=true, to_apply=%region_1.2 | all-reduce | flops 786432 | bytes 4718592 | tf_op jit(solution)/shard_map/psum | solution.py:120
  (59 shorter events, 14.6 us)
Async XLA Ops:
  7.2 25.5 %copy-start = (bf16[3,3,256,256]{3,2,1,0:T(8,128)(2,1)S(1)}, bf16[3,3,256,256]{3,2,1,0:T(8,128)(2,1)}, u32[]{:S(2)}) copy-start(bf16[3,3,256,256]{3,2,1,0:T(8,128)(2,1)} %param.14) | copy-start | bytes 3538948
  7.2 545.6 %all-reduce.4.cloned.1.call-start = ((), (), s32[]{:S(2)}) async-start(), calls=%async_computation | async-start | bytes 6291456 | tf_op jit(solution)/shard_map/psum | solution.py:120
  11.9 12.2 %collective-permute-start.3 = (f32[2,4,48,256]{3,0,2,1:T(2,128)}, f32[2,4,48,256]{3,0,2,1:T(2,128)}, u32[]{:S(2)}, u32[]{:S(2)}) collective-permute-start(f32[2,4,48,256]{3,0,2,1:T(2,128)} %copy.24), channel_id=1, source_target_pairs={{16,0},{32,16},{48,32},{64,48},{80,64},{96,80},{112,96},{128,112},... | collective-permute-start | bytes 1179656 | tf_op jit(solution)/shard_map/ppermute | solution.py:24
  25.9 6.8 copy-start.4
  36.8 14.4 %collective-permute-start.4 = (bf16[4,1,48,256]{3,2,1,0:T(8,128)(2,1)S(1)}, bf16[4,1,48,256]{3,2,1,0:T(8,128)(2,1)}, u32[]{:S(2)}, u32[]{:S(2)}) collective-permute-start(bf16[4,1,48,256]{3,2,1,0:T(8,128)(2,1)S(1)} %slice_bitcast_fusion.4), channel_id=1, source_target_pairs={{0,2},{2,4},{4,6},{6,8},{8,10},{10,12},{12,14},{1,3},{3,5},{5,7},{... | collective-permute-start | bytes 294920 | tf_op jit(solution)/shard_map/ppermute | solution.py:15
  47.9 17.2 %collective-permute-start.5 = (bf16[4,1,48,256]{3,2,1,0:T(8,128)(2,1)S(1)}, bf16[4,1,48,256]{3,2,1,0:T(8,128)(2,1)S(1)}, u32[]{:S(2)}, u32[]{:S(2)}) collective-permute-start(bf16[4,1,48,256]{3,2,1,0:T(8,128)(2,1)S(1)} %slice_bitcast_fusion.3), channel_id=1, source_target_pairs={{2,0},{4,2},{6,4},{8,6},{10,8},{12,10},{14,12},{3,1},{5,3},{7,5},{... | collective-permute-start | bytes 294920 | tf_op jit(solution)/shard_map/ppermute | solution.py:16
  50.7 15.4 %copy-start.1 = (bf16[1,4,4,48,256]{4,3,2,1,0:T(8,128)(2,1)S(1)}, bf16[1,4,4,48,256]{4,3,2,1,0:T(8,128)(2,1)}, u32[]{:S(2)}) copy-start(bf16[1,4,4,48,256]{4,3,2,1,0:T(8,128)(2,1)} %param.13) | copy-start | bytes 1179652
  50.7 15.4 %copy-start.2 = (bf16[1,4,4,48,256]{4,3,2,1,0:T(8,128)(2,1)S(1)}, bf16[1,4,4,48,256]{4,3,2,1,0:T(8,128)(2,1)}, u32[]{:S(2)}) copy-start(bf16[1,4,4,48,256]{4,3,2,1,0:T(8,128)(2,1)} %param.12) | copy-start | bytes 1179652
  67.3 5.4 collective-permute-start
  69.2 17.2 %collective-permute-start.1 = (bf16[4,1,48,256]{3,2,1,0:T(8,128)(2,1)S(1)}, bf16[4,1,48,256]{3,2,1,0:T(8,128)(2,1)S(1)}, u32[]{:S(2)}, u32[]{:S(2)}) collective-permute-start(bf16[4,1,48,256]{3,2,1,0:T(8,128)(2,1)S(1)} %get-tuple-element.67), channel_id=1, source_target_pairs={{2,0},{4,2},{6,4},{8,6},{10,8},{12,10},{14,12},{3,1},{5,3},{7,5},{... | collective-permute-start | bytes 294920 | tf_op jit(solution)/shard_map/ppermute | solution.py:16
  86.9 0.7 copy-start.5
  89.5 6.4 collective-permute-start.2
  98.6 1.0 copy-start.3
Sparse Core Ops, SparseCore 0:
  98.7 454.0 all-reduce.3
